TPU v7x, 256 devices: a whole 4x4x8 slice. The times are simulated.
256 devices in a mesh: replica: 16 (over z, core), mp: 16 (over y, x).
Axes of the slice: x: 4, y: 4, z: 8, core: 2. Of those that a mesh axis runs over, the one named last changes fastest.
Arguments:
- gradients: bfloat16 [16, 8, 768, 3072], P('replica', None, 'mp'), may hold values from -6 to 6
- feedback: bfloat16 [16, 8, 768, 3072], P('replica', None, 'mp'), may hold values from -4 to 4
- right_init: bfloat16 [8, 3072, 32], replicated, may hold values from -0.109375 to 0.109375
- gram_root: float32 [8, 32, 32], replicated, as said below
- owners: int32 [8], replicated, may hold values from 0 to 15, as said below
- momentum: float32 [16, 1, 768, 3072], P('mp', None, 'replica'), may hold values from -4 to 4
- master_weights: float32 [16, 1, 768, 3072], P('mp', None, 'replica'), may hold values from -1.5 to 1.5
- vector_grads: float32 [16, 10752], P('replica', 'mp'), may hold values from -6 to 6
- vector_momentum: float32 [10752], P('mp'), may hold values from -6 to 6
- vector_params: float32 [10752], P('mp'), may hold values from -6 to 6
Outputs:
- new_feedback: bfloat16 [16, 8, 768, 3072], P('replica', None, 'mp')
- new_momentum: float32 [16, 1, 768, 3072], P('mp', None, 'replica')
- new_master: float32 [16, 1, 768, 3072], P('mp', None, 'replica')
- new_weights: bfloat16 [8, 768, 3072], P(None, 'replica')
- new_vector_momentum: float32 [10752], P('mp')
- new_vector_params: float32 [10752], P('mp')
Inputs may be any that keep to these rules, and one draw needn't show every extreme that they name: `owners`: every matrix has one owner; no owner holds more than 1 of the 8 matrices, and one owner holds exactly 1. `gram_root`: each matrix is the identity plus off-diagonal terms, times a positive scale.
All inputs are finite; a program needn't handle non-finite values.
Results may differ from a plain program's by a relative error of at most 0.007.
Values may be sent and summed in bfloat16 or wider, within the bound.
A program may use at most 192 MiB of HBM per device.

v0:
```python
import jax
import jax.numpy as jnp
from jax import lax
from jax.sharding import PartitionSpec as P


def per_device(
    gradients,
    feedback,
    right_init,
    gram_root,
    owners,
    momentum,
    master_weights,
    vector_grads,
    vector_momentum,
    vector_params,
):
    highest = lax.Precision.HIGHEST
    compensated = (gradients[0].astype(jnp.float32) + feedback[0].astype(jnp.float32)).astype(
        jnp.bfloat16
    )
    owner_count = lax.axis_size("mp")
    capacity = momentum.shape[1]
    matrices = owners.shape[0]
    replica_rows = momentum.shape[2]
    mp_index = lax.axis_index("mp")
    replica_index = lax.axis_index("replica")
    same_owner = owners[:, None] == owners[None, :]
    earlier = jnp.arange(matrices)[:, None] < jnp.arange(matrices)[None, :]
    ranks = jnp.sum((same_owner & earlier).astype(jnp.int32), axis=0)
    slots = owners * capacity + ranks
    slot_table = (slots[None, :] == jnp.arange(owner_count * capacity)[:, None]).astype(jnp.float32)
    table_narrow = slot_table.astype(jnp.bfloat16)
    table_mine = lax.dynamic_slice_in_dim(slot_table, mp_index * capacity, capacity, 0)
    left_terms = jnp.einsum(
        "kmn,knr->kmr", compensated, right_init, preferred_element_type=jnp.float32
    )
    left_sum = lax.psum(left_terms, "replica")
    left_rows = jnp.einsum("kmr,krs->kms", left_sum, gram_root, precision=highest).astype(
        jnp.bfloat16
    )
    right_terms = jnp.einsum(
        "kmn,kms->kns", compensated, left_rows, preferred_element_type=jnp.float32
    )
    right_new = lax.psum(right_terms, ("replica", "mp"))
    left_all = lax.all_gather(left_rows, "mp", axis=1, tiled=True)
    approx_rows = jnp.einsum(
        "kms,kns->kmn", left_rows.astype(jnp.float32), right_new, precision=highest
    )
    new_feedback = (compensated.astype(jnp.float32) - approx_rows).astype(jnp.bfloat16)
    left_chosen = jnp.einsum(
        "ck,kmr->cmr", table_mine.astype(jnp.bfloat16), left_all, preferred_element_type=jnp.float32
    )
    left_chosen = lax.dynamic_slice_in_dim(
        left_chosen, replica_index * replica_rows, replica_rows, 1
    )
    right_chosen = jnp.einsum("ck,knr->cnr", table_mine, right_new, precision=highest)
    approx_slots = jnp.einsum("cmr,cnr->cmn", left_chosen, right_chosen, precision=highest)
    new_momentum = 0.9 * momentum[0] + approx_slots
    new_master = master_weights[0] - 0.1 * new_momentum
    master_narrow = new_master.astype(jnp.bfloat16)
    weight_slots = lax.all_gather(master_narrow, "mp", axis=0, tiled=True)
    new_weights = jnp.einsum(
        "sk,smn->kmn", table_narrow, weight_slots, preferred_element_type=jnp.float32
    ).astype(jnp.bfloat16)
    vector_total = lax.psum(vector_grads[0], "replica")
    new_vector_momentum = 0.9 * vector_momentum + vector_total
    new_vector_params = vector_params - 0.1 * new_vector_momentum
    return (
        new_feedback[None],
        new_momentum[None],
        new_master[None],
        new_weights,
        new_vector_momentum,
        new_vector_params,
    )


def solution(mesh):
    return jax.shard_map(
        per_device,
        mesh=mesh,
        in_specs=(
            P("replica", None, "mp", None),
            P("replica", None, "mp", None),
            P(),
            P(),
            P(),
            P("mp", None, "replica", None),
            P("mp", None, "replica", None),
            P("replica", "mp"),
            P("mp"),
            P("mp"),
        ),
        out_specs=(
            P("replica", None, "mp", None),
            P("mp", None, "replica", None),
            P("mp", None, "replica", None),
            P(None, "replica", None),
            P("mp"),
            P("mp"),
        ),
        check_vma=False,
    )
```

profile of v0, /device:TPU:1, one launch (start us, length us, event | category | flops | bytes accessed | tf_op | source)
XLA Modules:
  0.0 481.2 jit_solution(16211220204946410669)
XLA Ops:
  7.2 0.0 all-reduce.3.cloned.1.call-start
  7.2 0.8 reduce.1
  8.0 0.6 copy-done
  8.6 3.1 fusion.27
  11.8 50.5 %all-reduce = (f32[8,48,32]{1,2,0:T(8,128)S(1)}, f32[672]{0:T(1024)S(1)}) all-reduce(f32[8,48,32]{1,2,0:T(8,128)S(1)} %fusion.27, f32[672]{0:T(1024)S(1)} %reduce.1), channel_id=1, replica_groups=mesh['replica'=16,'mp'=16] {'replica'}, use_global_device_ids=true, to_apply=%region_0.0 | all-reduce | flops 12960 | bytes 103680 | tf_op jit(solution)/shard_map/psum | solution.py:39
  62.3 0.4 convolution_convert_fusion
  62.6 4.7 fusion.25
  67.4 0.0 all-gather.3.cloned.1.call-start
  67.4 0.1 copy.26
  67.6 0.4 copy-done.8
  68.0 0.1 convert_reduce_fusion
  68.1 22.7 %all_gather.6 = bf16[8,768,32]{2,0,1:T(8,128)(2,1)S(1)} all-gather(bf16[8,48,32]{2,0,1:T(8,128)(2,1)S(1)} %copy.26), channel_id=1, replica_groups=mesh['replica'=16,'mp'=16] {'mp'}, dimensions={1}, use_global_device_ids=true | all-gather | bytes 417792 | tf_op jit(solution)/shard_map/all_gather | solution.py:47
  90.8 1.1 multiply_reduce_fusion
  91.9 239.2 %all-reduce.3.cloned.1.call-done = f32[8,3072,32]{1,2,0:T(8,128)} async-done(((f32[8,3072,32]{1,2,0:T(8,128)}), f32[8,3072,32]{1,2,0:T(8,128)}) %all-reduce.3.cloned.1.call-update) | async-done | bytes 3145744 | tf_op jit(solution)/shard_map/psum | solution.py:46
  331.1 44.7 %fusion.6 = f32[1,3072,32]{0,1,2:T(8,128)} fusion(f32[8,3072,32]{1,2,0:T(8,128)} %all-reduce.3.cloned.1.call-done, pred[16,8]{1,0:T(8,128)(4,1)S(1)} %get-tuple-element.31, s32[]{:T(128)S(6)} %select_n.6), kind=kOutput, calls=%fused_computation.7 | convolution fusion | flops 9437184 | bytes 3539460 | tf_op jit(solution)/shard_map/ck,knr->cnr/dot_general | solution.py:58
  375.7 27.1 %copy.35 = f32[1,3072,32]{1,2,0:T(8,128)S(1)} copy(f32[1,3072,32]{0,1,2:T(8,128)} %fusion.6) | data formatting | bytes 786432 | tf_op jit(solution)/shard_map/ck,knr->cnr/dot_general | solution.py:58
  402.9 0.6 convolution_add_fusion
  403.6 1.2 fusion.10
  404.7 0.0 all-gather.3.cloned.1.call-update
  404.8 0.6 multiply_subtract_fusion
  405.4 7.4 %fusion.5 = bf16[1,8,48,3072]{3,2,1,0:T(8,128)(2,1)} fusion(bf16[8,48,32]{1,2,0:T(8,128)(2,1)S(1)} %convolution_convert_fusion, f32[8,3072,32]{1,2,0:T(8,128)} %all-reduce.3.cloned.1.call-done, bf16[1,8,48,3072]{3,2,1,0:T(8,128)(2,1)} %param.11, bf16[1,8,48,3072]{3,2,1,0:T(8,128)(2,1)} %param.10), kind=kOutput, calls=%fused_computation.5 | convolution fusion | flops 461242368 | bytes 10248192 | tf_op jit(solution)/shard_map/kms,kns->kmn/dot_general | solution.py:48
  412.8 51.4 %all-gather.3.cloned.1.call-done = bf16[768,3072]{1,0:T(8,128)(2,1)} async-done(((bf16[48,3072]{1,0:T(8,128)(2,1)}), bf16[768,3072]{1,0:T(8,128)(2,1)}) %all-gather.3.cloned.1.call-update) | async-done | bytes 4718608 | tf_op jit(solution)/shard_map/all_gather | solution.py:63
  464.2 7.5 %fusion.2 = bf16[8,48,3072]{2,0,1:T(8,128)(2,1)S(1)} fusion(bf16[16,48,3072]{2,1,0:T(8,128)(2,1)} %bitcast.41, s32[8]{0:T(128)S(1)} %add.27), kind=kOutput, calls=%fused_computation.4 | convolution fusion | flops 38928768 | bytes 7077920 | tf_op jit(solution)/shard_map/sk,smn->kmn/dot_general | solution.py:64
  471.7 2.7 copy.29
  (20 shorter events, 0.1 us)
Async XLA Ops:
  7.2 1.4 copy-start
  7.2 323.9 %all-reduce.3.cloned.1.call-start = ((), (), s32[]{:S(2)}) async-start(), calls=%async_computation | async-start | bytes 6291456 | tf_op jit(solution)/shard_map/psum | solution.py:46
  8.6 53.6 %copy-start.5 = (f32[8,32,32]{2,1,0:T(8,128)S(1)}, f32[8,32,32]{2,1,0:T(8,128)}, u32[]{:S(2)}) copy-start(f32[8,32,32]{2,1,0:T(8,128)} %param.13) | copy-start | bytes 98308
  67.3 0.7 copy-start.8
  67.4 396.9 %all-gather.3.cloned.1.call-start = ((), (), s32[]{:S(2)}) async-start(), calls=%async_computation.1 | async-start | bytes 5013504 | tf_op jit(solution)/shard_map/all_gather | solution.py:63
  375.7 27.1 %copy-start.3 = (f32[1,1,48,3072]{3,2,1,0:T(8,128)S(1)}, f32[1,1,48,3072]{3,2,1,0:T(8,128)}, u32[]{:S(2)}) copy-start(f32[1,1,48,3072]{3,2,1,0:T(8,128)} %param.15) | copy-start | bytes 1769476
  375.7 27.8 %copy-start.4 = (f32[1,1,48,3072]{3,2,1,0:T(8,128)S(1)}, f32[1,1,48,3072]{3,2,1,0:T(8,128)}, u32[]{:S(2)}) copy-start(f32[1,1,48,3072]{3,2,1,0:T(8,128)} %param.16) | copy-start | bytes 1769476
  402.9 1.9 copy-start.6
  402.9 1.9 copy-start.7
  403.6 9.2 %copy-start.2 = (f32[48,3072]{1,0:T(8,128)}, f32[48,3072]{1,0:T(8,128)S(1)}, u32[]{:S(2)}) copy-start(f32[48,3072]{1,0:T(8,128)S(1)} %convolution_add_fusion) | copy-start | bytes 1769476
  464.2 10.2 %copy-start.1 = (bf16[8,3072,32]{1,2,0:T(8,128)(2,1)S(1)}, bf16[8,3072,32]{1,2,0:T(8,128)(2,1)}, u32[]{:S(2)}) copy-start(bf16[8,3072,32]{1,2,0:T(8,128)(2,1)} %param.12) | copy-start | bytes 4718596
Sparse Core Ops, SparseCore 0:
  67.5 263.5 all-reduce.2
  404.9 59.2 all-gather.2
where the time goes:
time: 482 us; the launch traced here: 481 us
  waiting for transfers between devices  291 us (60%)
  blocking collectives  73.2 us (15%)
  matrix products  68.4 us (14%)
  local copies, waits for them, and re-layouts  31 us (6%)
  between operations  14.2 us (3%)
    psum x1, waiting for transfers between devices, per_device(): right_new = lax.psum(right_terms, ('replica', 'mp'))  239 us
    all_gather x1, waiting for transfers between devices, per_device(): weight_slots = lax.all_gather(master_narrow, 'mp', axis=0, tiled=True)  51.4 us
    psum x1, blocking collectives, per_device(): left_sum = lax.psum(left_terms, 'replica')  50.5 us
    dot_general x1, matrix products, per_device(): jnp.einsum('ck,knr->cnr', table_mine, right_new, precision=highest)  44.7 us
    dot_general x1, local copies, waits for them, and re-layouts, per_device(): jnp.einsum('ck,knr->cnr', table_mine, right_new, precision=highest)  27.1 us
    all_gather x1, blocking collectives, per_device(): left_all = lax.all_gather(left_rows, 'mp', axis=1, tiled=True)  22.7 us
  transfers between devices with their start and end apart: 2, of which 2 were waited for; matrix products, arithmetic and copies ran while one was open for 2% of the time, Pallas kernels for 0%

commit v1 on v0

--- a/solution.py
+++ b/solution.py
@@ -16,6 +16,28 @@
     vector_momentum,
     vector_params,
 ):
+
+    def rows_mix(inputs, ax_name, inner_x):
+        known = lax.axis_size(ax_name)
+        kept_rows = []
+        before, tile_out, fresh = (known, lax.axis_index(ax_name), inputs.shape[0])
+        for t in range(before):
+            kept_rows.append((t, (t + 1) % before))
+        vals = []
+        for t in range(before):
+            vals.append((t, (t - 1) % before))
+        local_out = before // 2
+        far_arr = step_out = inputs
+        z2 = inner_x(inputs, tile_out * fresh)
+        for k0 in range(1, local_out + 1):
+            far_arr = lax.ppermute(far_arr, axis_name=ax_name, perm=kept_rows)
+            if k0 < before - local_out:
+                step_out = lax.ppermute(step_out, axis_name=ax_name, perm=vals)
+                out_arr = inner_x(step_out, (tile_out + k0) % before * fresh)
+                z2 = z2 + out_arr
+            z2 = z2 + inner_x(far_arr, (tile_out - k0) % before * fresh)
+        return z2
+
     highest = lax.Precision.HIGHEST
     compensated = (gradients[0].astype(jnp.float32) + feedback[0].astype(jnp.float32)).astype(
         jnp.bfloat16
@@ -60,9 +82,15 @@
     new_momentum = 0.9 * momentum[0] + approx_slots
     new_master = master_weights[0] - 0.1 * new_momentum
     master_narrow = new_master.astype(jnp.bfloat16)
-    weight_slots = lax.all_gather(master_narrow, "mp", axis=0, tiled=True)
-    new_weights = jnp.einsum(
-        "sk,smn->kmn", table_narrow, weight_slots, preferred_element_type=jnp.float32
+    new_weights = rows_mix(
+        master_narrow,
+        "mp",
+        lambda own_block, offset: jnp.einsum(
+            "sk,smn->kmn",
+            lax.dynamic_slice_in_dim(table_narrow, offset, own_block.shape[0], axis=0),
+            own_block,
+            preferred_element_type=jnp.float32,
+        ),
     ).astype(jnp.bfloat16)
     vector_total = lax.psum(vector_grads[0], "replica")
     new_vector_momentum = 0.9 * vector_momentum + vector_total

time: 482 us -> 513 us (1.064); the launches traced: 481 us -> 505 us
  starting transfers between devices: 0.08 us -> 34.7 us
  waiting for transfers between devices: 291 us -> 282 us
  other arithmetic: 3.8 us -> 12.1 us
  matrix products: 68.4 us -> 60.2 us
    all_gather x1 -> x0, waiting for transfers between devices: 51.4 us -> none  [per_device(): weight_slots = lax.all_gather(master_narrow, 'mp', axis=0, tiled=True)]
    ppermute x0 -> x15, waiting for transfers between devices: none -> 44 us  [the longest x8 40.2 us: rows_mix(): far_arr = lax.ppermute(far_arr, axis_name=ax_name, perm=kept_rows)]
    ppermute x0 -> x15, starting transfers between devices: none -> 34.7 us  [the longest x7 33.4 us: rows_mix(): step_out = lax.ppermute(step_out, axis_name=ax_name, perm=vals)]
    dot_general x1 -> x0, matrix products: 7.46 us -> none  [per_device(): jnp.einsum('sk,smn->kmn', table_narrow, weight_slots, preferred_element_t...]
    convert_element_type x2, other arithmetic: 1.17 us -> 7.69 us  [the longest x1 7.68 us: per_device(): new_weights = rows_mix(master_narrow, 'mp', lambda own_block, offset: jnp...]
  transfers between devices with their start and end apart: 2 -> 16, of which waited for: 2 -> 9; matrix products, arithmetic and copies ran while one was open for 2% -> 2% of each run, Pallas kernels for 0% -> 0%
where the time goes in v1:
time: 513 us; the launch traced here: 505 us
  waiting for transfers between devices  282 us (55%)
  blocking collectives  73.4 us (14%)
  matrix products  60.2 us (12%)
  starting transfers between devices  34.7 us (7%)
  local copies, waits for them, and re-layouts  27.9 us (5%)
  between operations  14.7 us (3%)
  other arithmetic  12.1 us (2%)
    psum x1, waiting for transfers between devices, per_device(): right_new = lax.psum(right_terms, ('replica', 'mp'))  238 us
    psum x1, blocking collectives, per_device(): left_sum = lax.psum(left_terms, 'replica')  50.5 us
    dot_general x1, matrix products, per_device(): jnp.einsum('ck,knr->cnr', table_mine, right_new, precision=highest)  44.6 us
    ppermute x8, waiting for transfers between devices, rows_mix(): far_arr = lax.ppermute(far_arr, axis_name=ax_name, perm=kept_rows)  40.2 us
    ppermute x7, starting transfers between devices, rows_mix(): step_out = lax.ppermute(step_out, axis_name=ax_name, perm=vals)  33.4 us
    dot_general x1, local copies, waits for them, and re-layouts, per_device(): jnp.einsum('ck,knr->cnr', table_mine, right_new, precision=highest)  27.1 us
    all_gather x1, blocking collectives, per_device(): left_all = lax.all_gather(left_rows, 'mp', axis=1, tiled=True)  22.9 us
  transfers between devices with their start and end apart: 16, of which 9 were waited for; matrix products, arithmetic and copies ran while one was open for 2% of the time, Pallas kernels for 0%

profile of v1, /device:TPU:1, one launch (start us, length us, event | category | flops | bytes accessed | tf_op | source)
XLA Modules:
  0.0 505.3 jit_solution(5625127664454672344)
XLA Ops:
  8.6 3.1 fusion.50
  11.7 50.5 %all-reduce = (f32[8,48,32]{1,2,0:T(8,128)S(1)}, f32[672]{0:T(1024)S(1)}) all-reduce(f32[8,48,32]{1,2,0:T(8,128)S(1)} %fusion.50, f32[672]{0:T(1024)S(1)} %reduce.1), channel_id=1, replica_groups=mesh['replica'=16,'mp'=16] {'replica'}, use_global_device_ids=true, to_apply=%region_0.0 | all-reduce | flops 12960 | bytes 103680 | tf_op jit(solution)/shard_map/psum | solution.py:61
  62.6 4.7 fusion.48
  67.9 22.9 %all_gather.3 = bf16[8,768,32]{2,0,1:T(8,128)(2,1)S(1)} all-gather(bf16[8,48,32]{2,0,1:T(8,128)(2,1)S(1)} %copy.20), channel_id=1, replica_groups=mesh['replica'=16,'mp'=16] {'mp'}, dimensions={1}, use_global_device_ids=true | all-gather | bytes 417792 | tf_op jit(solution)/shard_map/all_gather | solution.py:69
  92.7 238.4 %all-reduce.3.cloned.1.call-done = f32[8,3072,32]{1,2,0:T(8,128)} async-done(((f32[8,3072,32]{1,2,0:T(8,128)}), f32[8,3072,32]{1,2,0:T(8,128)}) %all-reduce.3.cloned.1.call-update) | async-done | bytes 3145744 | tf_op jit(solution)/shard_map/psum | solution.py:68
  331.0 44.6 %fusion.1 = f32[1,3072,32]{0,1,2:T(8,128)} fusion(f32[8,3072,32]{1,2,0:T(8,128)} %all-reduce.3.cloned.1.call-done, pred[16,8]{1,0:T(8,128)(4,1)S(1)} %get-tuple-element.31, s32[]{:T(128)S(6)} %select_n.115), kind=kOutput, calls=%fused_computation.5 | convolution fusion | flops 9437184 | bytes 3539460 | tf_op jit(solution)/shard_map/ck,knr->cnr/dot_general | solution.py:80
  375.7 27.1 %copy.26 = f32[1,3072,32]{1,2,0:T(8,128)S(1)} copy(f32[1,3072,32]{0,1,2:T(8,128)} %fusion.1) | data formatting | bytes 786432 | tf_op jit(solution)/shard_map/ck,knr->cnr/dot_general | solution.py:80
  404.6 1.2 collective-permute-start.1
  405.8 3.6 collective-permute-start
  409.4 6.7 %fusion = bf16[1,8,48,3072]{3,2,1,0:T(8,128)(2,1)} fusion(bf16[8,48,32]{1,2,0:T(8,128)(2,1)S(1)} %convolution_convert_fusion, f32[8,3072,32]{1,2,0:T(8,128)} %all-reduce.3.cloned.1.call-done, bf16[1,8,48,3072]{3,2,1,0:T(8,128)(2,1)S(1)} %copy-done.2, bf16[1,8,48,3072]{3,2,1,0:T(8,128)(2,1)} %param.10), kind=kOutput, calls=%fused_computation.3 | convolution fusion | flops 461242368 | bytes 10248192 | tf_op jit(solution)/shard_map/kms,kns->kmn/dot_general | solution.py:70
  416.2 4.8 collective-permute-start.2
  421.1 3.9 collective-permute-done.3
  425.1 4.9 collective-permute-start.4
  430.0 3.6 collective-permute-done.4
  433.6 5.2 %collective-permute-start.6 = (bf16[1,48,3072]{2,1,0:T(8,128)(2,1)S(1)}, bf16[1,48,3072]{2,1,0:T(8,128)(2,1)S(1)}, u32[]{:S(2)}, u32[]{:S(2)}) collective-permute-start(bf16[1,48,3072]{2,1,0:T(8,128)(2,1)S(1)} %collective-permute-done.4), channel_id=1, source_target_pairs={{0,15},{1,0},{2,1},{3,2},{4,3},{5,4},{6,5},{7,6},{8,7},{9,8},{10,9... | collective-permute-start | bytes 884744 | tf_op jit(solution)/shard_map/ppermute | solution.py:35
  439.0 8.8 %collective-permute-done.7 = bf16[1,48,3072]{2,1,0:T(8,128)(2,1)S(1)} collective-permute-done((bf16[1,48,3072]{2,1,0:T(8,128)(2,1)S(1)}, bf16[1,48,3072]{2,1,0:T(8,128)(2,1)S(1)}, u32[]{:S(2)}, u32[]{:S(2)}) %collective-permute-start.7) | collective-permute-done | bytes 294944 | tf_op jit(solution)/shard_map/ppermute | solution.py:33
  447.9 4.9 collective-permute-start.8
  452.8 4.3 collective-permute-done.9
  457.1 4.9 collective-permute-start.10
  462.1 5.4 %collective-permute-done.11 = bf16[1,48,3072]{2,1,0:T(8,128)(2,1)S(1)} collective-permute-done((bf16[1,48,3072]{2,1,0:T(8,128)(2,1)S(1)}, bf16[1,48,3072]{2,1,0:T(8,128)(2,1)S(1)}, u32[]{:S(2)}, u32[]{:S(2)}) %collective-permute-start.11) | collective-permute-done | bytes 294944 | tf_op jit(solution)/shard_map/ppermute | solution.py:33
  467.5 5.1 %collective-permute-start.12 = (bf16[1,48,3072]{2,1,0:T(8,128)(2,1)S(1)}, bf16[1,48,3072]{2,1,0:T(8,128)(2,1)S(1)}, u32[]{:S(2)}, u32[]{:S(2)}) collective-permute-start(bf16[1,48,3072]{2,1,0:T(8,128)(2,1)S(1)} %collective-permute-done.10), channel_id=1, source_target_pairs={{0,15},{1,0},{2,1},{3,2},{4,3},{5,4},{6,5},{7,6},{8,7},{9,8},{10,9... | collective-permute-start | bytes 884744 | tf_op jit(solution)/shard_map/ppermute | solution.py:35
  472.7 6.2 %collective-permute-done.13 = bf16[1,48,3072]{2,1,0:T(8,128)(2,1)S(1)} collective-permute-done((bf16[1,48,3072]{2,1,0:T(8,128)(2,1)S(1)}, bf16[1,48,3072]{2,1,0:T(8,128)(2,1)S(1)}, u32[]{:S(2)}, u32[]{:S(2)}) %collective-permute-start.13) | collective-permute-done | bytes 294944 | tf_op jit(solution)/shard_map/ppermute | solution.py:33
  479.1 11.6 %collective-permute-done.14 = bf16[1,48,3072]{2,1,0:T(8,128)(2,1)S(1)} collective-permute-done((bf16[1,48,3072]{2,1,0:T(8,128)(2,1)S(1)}, bf16[1,48,3072]{2,1,0:T(8,128)(2,1)S(1)}, u32[]{:S(2)}, u32[]{:S(2)}) %collective-permute-start.14) | collective-permute-done | bytes 294944 | tf_op jit(solution)/shard_map/ppermute | solution.py:33
  490.8 7.7 %add_convert_fusion = bf16[8,48,3072]{2,1,0:T(8,128)(2,1)} fusion(f32[48,3072]{1,0:T(8,128)S(1)} %bitcast_convert_fusion, f32[8]{0:T(128)S(1)} %get-tuple-element.14, f32[48,3072]{1,0:T(8,128)S(1)} %bitcast_convert_fusion.1, f32[8]{0:T(128)S(1)} %get-tuple-element.15, f32[48,3072]{1,0:T(8,128)S(1)} %bitcast_convert_fusion.2, f32[8]{0:T(128)S(1)} %get-tuple-element.16, ...), kind=kLoop, calls=%fused_computation | loop fusion | flops 37748736 | bytes 11796992 | tf_op jit(solution)/shard_map/convert_element_type | solution.py:94
  (64 shorter events, 6.6 us)
Async XLA Ops:
  7.2 55.0 %copy-start.6 = (f32[8,32,32]{2,1,0:T(8,128)S(1)}, f32[8,32,32]{2,1,0:T(8,128)}, u32[]{:S(2)}) copy-start(f32[8,32,32]{2,1,0:T(8,128)} %param.13) | copy-start | bytes 98308
  7.2 323.9 %all-reduce.3.cloned.1.call-start = ((), (), s32[]{:S(2)}) async-start(), calls=%async_computation | async-start | bytes 6291456 | tf_op jit(solution)/shard_map/psum | solution.py:68
  67.3 24.7 %copy-start.7 = (f32[672]{0:T(1024)S(1)}, f32[672]{0:T(1024)}, u32[]{:S(2)}) copy-start(f32[672]{0:T(1024)} %param.19) | copy-start | bytes 8068
  67.3 24.7 %copy-start.8 = (f32[672]{0:T(1024)S(1)}, f32[672]{0:T(1024)}, u32[]{:S(2)}) copy-start(f32[672]{0:T(1024)} %param.18) | copy-start | bytes 8068
  375.7 27.1 %copy-start.4 = (f32[1,1,48,3072]{3,2,1,0:T(8,128)S(1)}, f32[1,1,48,3072]{3,2,1,0:T(8,128)}, u32[]{:S(2)}) copy-start(f32[1,1,48,3072]{3,2,1,0:T(8,128)} %param.15) | copy-start | bytes 1769476
  375.7 27.8 %copy-start.5 = (f32[1,1,48,3072]{3,2,1,0:T(8,128)S(1)}, f32[1,1,48,3072]{3,2,1,0:T(8,128)}, u32[]{:S(2)}) copy-start(f32[1,1,48,3072]{3,2,1,0:T(8,128)} %param.16) | copy-start | bytes 1769476
  402.8 6.6 %copy-start.2 = (bf16[1,8,48,3072]{3,2,1,0:T(8,128)(2,1)S(1)}, bf16[1,8,48,3072]{3,2,1,0:T(8,128)(2,1)}, u32[]{:S(2)}) copy-start(bf16[1,8,48,3072]{3,2,1,0:T(8,128)(2,1)} %param.11) | copy-start | bytes 7077892
  403.5 12.6 %copy-start.3 = (f32[48,3072]{1,0:T(8,128)}, f32[48,3072]{1,0:T(8,128)S(1)}, u32[]{:S(2)}) copy-start(f32[48,3072]{1,0:T(8,128)S(1)} %convolution_add_fusion) | copy-start | bytes 1769476
  404.6 11.5 %collective-permute-start.1 = (bf16[1,48,3072]{2,1,0:T(8,128)(2,1)S(1)}, bf16[1,48,3072]{2,1,0:T(8,128)(2,1)S(1)}, u32[]{:S(2)}, u32[]{:S(2)}) collective-permute-start(bf16[1,48,3072]{2,1,0:T(8,128)(2,1)S(1)} %bitcast.165), channel_id=1, source_target_pairs={{0,1},{1,2},{2,3},{3,4},{4,5},{5,6},{6,7},{7,8},{8,9},{9,10},{10,1... | collective-permute-start | bytes 884744 | tf_op jit(solution)/shard_map/ppermute | solution.py:33
  405.8 10.4 %collective-permute-start = (bf16[1,48,3072]{2,1,0:T(8,128)(2,1)S(1)}, bf16[1,48,3072]{2,1,0:T(8,128)(2,1)S(1)}, u32[]{:S(2)}, u32[]{:S(2)}) collective-permute-start(bf16[1,48,3072]{2,1,0:T(8,128)(2,1)S(1)} %bitcast.166), channel_id=1, source_target_pairs={{0,15},{1,0},{2,1},{3,2},{4,3},{5,4},{6,5},{7,6},{8,7},{9,8},{10,9... | collective-permute-start | bytes 884744 | tf_op jit(solution)/shard_map/ppermute | solution.py:35
  416.1 8.9 %collective-permute-start.3 = (bf16[1,48,3072]{2,1,0:T(8,128)(2,1)S(1)}, bf16[1,48,3072]{2,1,0:T(8,128)(2,1)S(1)}, u32[]{:S(2)}, u32[]{:S(2)}) collective-permute-start(bf16[1,48,3072]{2,1,0:T(8,128)(2,1)S(1)} %collective-permute-done.1), channel_id=1, source_target_pairs={{0,1},{1,2},{2,3},{3,4},{4,5},{5,6},{6,7},{7,8},{8,9},{9,10},{10,1... | collective-permute-start | bytes 884744 | tf_op jit(solution)/shard_map/ppermute | solution.py:33
  416.2 8.9 %collective-permute-start.2 = (bf16[1,48,3072]{2,1,0:T(8,128)(2,1)S(1)}, bf16[1,48,3072]{2,1,0:T(8,128)(2,1)S(1)}, u32[]{:S(2)}, u32[]{:S(2)}) collective-permute-start(bf16[1,48,3072]{2,1,0:T(8,128)(2,1)S(1)} %collective-permute-done), channel_id=1, source_target_pairs={{0,15},{1,0},{2,1},{3,2},{4,3},{5,4},{6,5},{7,6},{8,7},{9,8},{10,9... | collective-permute-start | bytes 884744 | tf_op jit(solution)/shard_map/ppermute | solution.py:35
  425.0 13.9 %collective-permute-start.5 = (bf16[1,48,3072]{2,1,0:T(8,128)(2,1)S(1)}, bf16[1,48,3072]{2,1,0:T(8,128)(2,1)S(1)}, u32[]{:S(2)}, u32[]{:S(2)}) collective-permute-start(bf16[1,48,3072]{2,1,0:T(8,128)(2,1)S(1)} %collective-permute-done.3), channel_id=1, source_target_pairs={{0,1},{1,2},{2,3},{3,4},{4,5},{5,6},{6,7},{7,8},{8,9},{9,10},{10,1... | collective-permute-start | bytes 884744 | tf_op jit(solution)/shard_map/ppermute | solution.py:33
  425.1 8.5 %collective-permute-start.4 = (bf16[1,48,3072]{2,1,0:T(8,128)(2,1)S(1)}, bf16[1,48,3072]{2,1,0:T(8,128)(2,1)S(1)}, u32[]{:S(2)}, u32[]{:S(2)}) collective-permute-start(bf16[1,48,3072]{2,1,0:T(8,128)(2,1)S(1)} %collective-permute-done.2), channel_id=1, source_target_pairs={{0,15},{1,0},{2,1},{3,2},{4,3},{5,4},{6,5},{7,6},{8,7},{9,8},{10,9... | collective-permute-start | bytes 884744 | tf_op jit(solution)/shard_map/ppermute | solution.py:35
  433.6 14.3 %collective-permute-start.6 = (bf16[1,48,3072]{2,1,0:T(8,128)(2,1)S(1)}, bf16[1,48,3072]{2,1,0:T(8,128)(2,1)S(1)}, u32[]{:S(2)}, u32[]{:S(2)}) collective-permute-start(bf16[1,48,3072]{2,1,0:T(8,128)(2,1)S(1)} %collective-permute-done.4), channel_id=1, source_target_pairs={{0,15},{1,0},{2,1},{3,2},{4,3},{5,4},{6,5},{7,6},{8,7},{9,8},{10,9... | collective-permute-start | bytes 884744 | tf_op jit(solution)/shard_map/ppermute | solution.py:35
  438.9 9.0 %collective-permute-start.7 = (bf16[1,48,3072]{2,1,0:T(8,128)(2,1)S(1)}, bf16[1,48,3072]{2,1,0:T(8,128)(2,1)S(1)}, u32[]{:S(2)}, u32[]{:S(2)}) collective-permute-start(bf16[1,48,3072]{2,1,0:T(8,128)(2,1)S(1)} %collective-permute-done.5), channel_id=1, source_target_pairs={{0,1},{1,2},{2,3},{3,4},{4,5},{5,6},{6,7},{7,8},{8,9},{9,10},{10,1... | collective-permute-start | bytes 884744 | tf_op jit(solution)/shard_map/ppermute | solution.py:33
  447.8 9.2 %collective-permute-start.9 = (bf16[1,48,3072]{2,1,0:T(8,128)(2,1)S(1)}, bf16[1,48,3072]{2,1,0:T(8,128)(2,1)S(1)}, u32[]{:S(2)}, u32[]{:S(2)}) collective-permute-start(bf16[1,48,3072]{2,1,0:T(8,128)(2,1)S(1)} %collective-permute-done.7), channel_id=1, source_target_pairs={{0,1},{1,2},{2,3},{3,4},{4,5},{5,6},{6,7},{7,8},{8,9},{9,10},{10,1... | collective-permute-start | bytes 884744 | tf_op jit(solution)/shard_map/ppermute | solution.py:33
  447.9 9.2 %collective-permute-start.8 = (bf16[1,48,3072]{2,1,0:T(8,128)(2,1)S(1)}, bf16[1,48,3072]{2,1,0:T(8,128)(2,1)S(1)}, u32[]{:S(2)}, u32[]{:S(2)}) collective-permute-start(bf16[1,48,3072]{2,1,0:T(8,128)(2,1)S(1)} %collective-permute-done.6), channel_id=1, source_target_pairs={{0,15},{1,0},{2,1},{3,2},{4,3},{5,4},{6,5},{7,6},{8,7},{9,8},{10,9... | collective-permute-start | bytes 884744 | tf_op jit(solution)/shard_map/ppermute | solution.py:35
  457.1 10.3 %collective-permute-start.11 = (bf16[1,48,3072]{2,1,0:T(8,128)(2,1)S(1)}, bf16[1,48,3072]{2,1,0:T(8,128)(2,1)S(1)}, u32[]{:S(2)}, u32[]{:S(2)}) collective-permute-start(bf16[1,48,3072]{2,1,0:T(8,128)(2,1)S(1)} %collective-permute-done.9), channel_id=1, source_target_pairs={{0,1},{1,2},{2,3},{3,4},{4,5},{5,6},{6,7},{7,8},{8,9},{9,10},{10,1... | collective-permute-start | bytes 884744 | tf_op jit(solution)/shard_map/ppermute | solution.py:33
  457.1 10.3 %collective-permute-start.10 = (bf16[1,48,3072]{2,1,0:T(8,128)(2,1)S(1)}, bf16[1,48,3072]{2,1,0:T(8,128)(2,1)S(1)}, u32[]{:S(2)}, u32[]{:S(2)}) collective-permute-start(bf16[1,48,3072]{2,1,0:T(8,128)(2,1)S(1)} %collective-permute-done.8), channel_id=1, source_target_pairs={{0,15},{1,0},{2,1},{3,2},{4,3},{5,4},{6,5},{7,6},{8,7},{9,8},{10,9... | collective-permute-start | bytes 884744 | tf_op jit(solution)/shard_map/ppermute | solution.py:35
  467.4 11.4 %collective-permute-start.13 = (bf16[1,48,3072]{2,1,0:T(8,128)(2,1)S(1)}, bf16[1,48,3072]{2,1,0:T(8,128)(2,1)S(1)}, u32[]{:S(2)}, u32[]{:S(2)}) collective-permute-start(bf16[1,48,3072]{2,1,0:T(8,128)(2,1)S(1)} %collective-permute-done.11), channel_id=1, source_target_pairs={{0,1},{1,2},{2,3},{3,4},{4,5},{5,6},{6,7},{7,8},{8,9},{9,10},{10,1... | collective-permute-start | bytes 884744 | tf_op jit(solution)/shard_map/ppermute | solution.py:33
  467.5 11.6 %collective-permute-start.12 = (bf16[1,48,3072]{2,1,0:T(8,128)(2,1)S(1)}, bf16[1,48,3072]{2,1,0:T(8,128)(2,1)S(1)}, u32[]{:S(2)}, u32[]{:S(2)}) collective-permute-start(bf16[1,48,3072]{2,1,0:T(8,128)(2,1)S(1)} %collective-permute-done.10), channel_id=1, source_target_pairs={{0,15},{1,0},{2,1},{3,2},{4,3},{5,4},{6,5},{7,6},{8,7},{9,8},{10,9... | collective-permute-start | bytes 884744 | tf_op jit(solution)/shard_map/ppermute | solution.py:35
  478.8 11.9 %collective-permute-start.14 = (bf16[1,48,3072]{2,1,0:T(8,128)(2,1)S(1)}, bf16[1,48,3072]{2,1,0:T(8,128)(2,1)S(1)}, u32[]{:S(2)}, u32[]{:S(2)}) collective-permute-start(bf16[1,48,3072]{2,1,0:T(8,128)(2,1)S(1)} %collective-permute-done.13), channel_id=1, source_target_pairs={{0,1},{1,2},{2,3},{3,4},{4,5},{5,6},{6,7},{7,8},{8,9},{9,10},{10,1... | collective-permute-start | bytes 884744 | tf_op jit(solution)/shard_map/ppermute | solution.py:33
  490.8 7.7 %copy-start.1 = (bf16[8,3072,32]{1,2,0:T(8,128)(2,1)S(1)}, bf16[8,3072,32]{1,2,0:T(8,128)(2,1)}, u32[]{:S(2)}) copy-start(bf16[8,3072,32]{1,2,0:T(8,128)(2,1)} %param.12) | copy-start | bytes 4718596
  (2 other events, 6.6 us)
Sparse Core Ops, SparseCore 0:
  67.5 263.5 all-reduce.2
